TPU v7x, 128 devices: a whole 4x4x4 slice. The times are simulated.
128 devices in a mesh: req: 4 (over z), tile: 8 (over y, core), span: 4 (over x).
Axes of the slice: x: 4, y: 4, z: 4, core: 2. Of those that a mesh axis runs over, the one named last changes fastest.
Arguments:
- latents: bfloat16 [32, 64, 128, 512], P(('req', 'span'), 'tile'), may hold values from -12 to 12
- frame_counts: int32 [4], replicated, may hold values from 1 to 16, 32 in all
- norm_gain: float32 [512], replicated, may hold values from 0.1 to 1.9
- norm_shift: float32 [512], replicated, may hold values from -3 to 3
- conv_weight: bfloat16 [3, 3, 3, 512, 512], replicated, may hold values from -0.0546875 to 0.0546875
- conv_bias: float32 [512], replicated, may hold values from -2 to 2
Outputs:
- decoded: bfloat16 [32, 64, 128, 512], P(('req', 'span'), 'tile')
Inputs may be any that keep to these rules, and one draw needn't show every extreme that they name: `frame_counts`: the 4 counts sum to 32, and the largest is exactly 16.
All inputs are finite; a program needn't handle non-finite values.
Results may differ from a plain program's by a relative error of at most 0.0031.
Values may be sent and summed in bfloat16 or wider, within the bound.
No kernel may reach another device: no remote copies, remote signals or barrier semaphores. Data moves between devices by JAX's collectives and lax.ppermute only.
A program may use at most 192 MiB of HBM per device.

v0:
```python
import jax
import jax.numpy as jnp
from jax import lax
from jax.sharding import PartitionSpec as P

GROUPS = 32
EPSILON = 1e-06


def extended_2(array, sides, width):
    for axis, dim in sides:
        count, length = (lax.axis_size(axis), array.shape[dim])
        up = [(i, (i + 1) % count) for i in range(count - 1)]
        down = [(j, i) for i, j in up]
        last = lax.slice_in_dim(array, length - width, length, axis=dim)
        leading = lax.slice_in_dim(array, 0, width, axis=dim)
        before = lax.ppermute(last, axis, up)
        after = lax.ppermute(leading, axis, down)
        array = jnp.concatenate([before, array, after], axis=dim)
    return array


def shifted(array, axis, by):
    count = lax.axis_size(axis)
    pairs = [(i, i + by) for i in range(count) if 0 <= i + by < count]
    return lax.ppermute(array, axis, pairs)


def membership(positions, request_start, request_end):
    return (positions[:, None] >= request_start[None, :]) & (
        positions[:, None] < request_end[None, :]
    )


def normalize(
    source, positions, request_start, request_end, group_mean, group_scale, norm_gain, norm_shift
):
    inside = membership(positions, request_start, request_end).astype(jnp.float32)
    per_group = source.shape[-1] // group_mean.shape[1]
    frame_mean = jnp.repeat(
        jnp.dot(inside, group_mean, precision=lax.Precision.HIGHEST), per_group, axis=1
    )
    frame_scale = jnp.repeat(
        jnp.dot(inside, group_scale, precision=lax.Precision.HIGHEST), per_group, axis=1
    )
    centred = (source.astype(jnp.float32) - frame_mean[:, None, None, :]) * frame_scale[
        :, None, None, :
    ]
    return jax.nn.silu(centred * norm_gain + norm_shift).astype(jnp.bfloat16)


def finish_stats(local_sums, local_squares, cell_count):
    total_sums, total_squares = lax.psum((local_sums, local_squares), ("req", "tile", "span"))
    group_mean = total_sums / cell_count
    group_scale = lax.rsqrt(total_squares / cell_count - group_mean * group_mean + EPSILON)
    return (group_mean, group_scale)


def extend_rows(source):
    haloed = extended_2(source, (("tile", 1),), 1)
    tile_place = lax.axis_index("tile")
    upper_rim = jnp.where(tile_place == 0, haloed[:, 1:2], haloed[:, 0:1])
    bottom = jnp.where(tile_place == lax.axis_size("tile") - 1, haloed[:, -2:-1], haloed[:, -1:])
    return jnp.concatenate([upper_rim, haloed[:, 1:-1], bottom], axis=1)


def extend_frames(source):
    earlier = shifted(source, ("req", "span"), 1)
    return jnp.concatenate([earlier, source], axis=0)


def extend(source):
    grown = extend_rows(extend_frames(source))
    return grown


def convolve(padded, tap_index, conv_weight, frame_count, row_count, col_count, channels):
    accumulated = jnp.zeros((frame_count * row_count * col_count, channels), jnp.float32)
    for time_tap in range(3):
        chosen = jnp.take(padded, tap_index[time_tap], axis=0)
        for row_tap in range(3):
            stacked = jnp.concatenate(
                [
                    chosen[:, row_tap : row_tap + row_count, col_tap : col_tap + col_count]
                    for col_tap in range(3)
                ],
                axis=-1,
            )
            kernel = conv_weight[time_tap, row_tap].reshape(3 * channels, channels)
            accumulated = accumulated + jnp.dot(
                stacked.reshape(frame_count * row_count * col_count, 3 * channels),
                kernel,
                preferred_element_type=jnp.float32,
            )
    return accumulated.reshape(frame_count, row_count, col_count, channels)


def shards(latents, frame_counts, norm_gain, norm_shift, conv_weight, conv_bias):
    frame_count, row_count, col_count, channels = latents.shape
    per_group = channels // GROUPS
    request_end = jnp.cumsum(frame_counts)
    request_start = request_end - frame_counts
    first_frame = lax.axis_index(("req", "span")) * frame_count
    positions = first_frame + jnp.arange(frame_count, dtype=jnp.int32)
    inside = membership(positions, request_start, request_end)
    values = latents.astype(jnp.float32)
    group_sums = jnp.sum(values, axis=(1, 2)).reshape(frame_count, GROUPS, per_group).sum(-1)
    group_squares = (
        jnp.sum(values * values, axis=(1, 2)).reshape(frame_count, GROUPS, per_group).sum(-1)
    )
    weights_in = inside.astype(jnp.float32)
    local_sums = jnp.dot(weights_in.T, group_sums, precision=lax.Precision.HIGHEST)
    local_squares = jnp.dot(weights_in.T, group_squares, precision=lax.Precision.HIGHEST)
    cell_count = (
        frame_counts * (row_count * lax.axis_size("tile") * col_count * per_group)
    ).astype(jnp.float32)[:, None]
    group_mean, group_scale = finish_stats(local_sums, local_squares, cell_count)
    hidden = normalize(
        latents,
        positions,
        request_start,
        request_end,
        group_mean,
        group_scale,
        norm_gain,
        norm_shift,
    )
    extended = extend(hidden)
    padded = jnp.pad(extended, ((0, 0), (0, 0), (1, 1), (0, 0)), mode="edge")
    frame_start = jnp.sum(jnp.where(inside, request_start[None, :], 0), axis=1)
    tap_index = jnp.stack(
        [
            jnp.maximum(positions - 2 + time_tap, frame_start) - first_frame + 2
            for time_tap in range(3)
        ],
        axis=0,
    )
    conv = convolve(padded, tap_index, conv_weight, frame_count, row_count, col_count, channels)
    return (values + conv + conv_bias).astype(jnp.bfloat16)


def solution(mesh):
    placed = (P(("req", "span"), "tile", None, None), P(), P(), P(), P(), P())
    return jax.shard_map(
        shards,
        mesh=mesh,
        in_specs=placed,
        out_specs=P(("req", "span"), "tile", None, None),
        check_vma=False,
    )
```

profile of v0, /device:TPU:41, one launch (start us, length us, event | category | flops | bytes accessed | tf_op | source)
XLA Modules:
  0.0 287.2 jit_solution(3329410029690608245)
XLA Ops:
  4.6 65.0 %all-reduce = (f32[4,32]{1,0:T(4,128)S(1)}, f32[4,32]{1,0:T(4,128)S(1)}) all-reduce(f32[4,32]{1,0:T(4,128)S(1)} %fusion.40, f32[4,32]{1,0:T(4,128)S(1)} %fusion.39), channel_id=1, replica_groups=mesh['req'=4,'tile'=8,'span'=4] {'req','tile','span'}, use_global_device_ids=true, to_apply=%region_6.7 | all-reduce | flops 256 | bytes 2048 | tf_op jit(solution)/shard_map/psum | solution.py:53
  75.3 48.6 %collective-permute-done = bf16[2,8,128,512]{3,2,1,0:T(8,128)(2,1)} collective-permute-done((bf16[2,8,128,512]{3,2,1,0:T(8,128)(2,1)S(1)}, bf16[2,8,128,512]{3,2,1,0:T(8,128)(2,1)}, u32[]{:S(2)}, u32[]{:S(2)}) %collective-permute-start) | collective-permute-done | bytes 2097184 | tf_op jit(solution)/shard_map/ppermute | solution.py:26
  124.9 4.4 %collective-permute-start.1 = (bf16[4,1,128,512]{3,2,1,0:T(8,128)(2,1)S(1)}, bf16[4,1,128,512]{3,2,1,0:T(8,128)(2,1)S(1)}, u32[]{:S(2)}, u32[]{:S(2)}) collective-permute-start(bf16[4,1,128,512]{3,2,1,0:T(8,128)(2,1)S(1)} %pad_maximum_fusion.9), channel_id=1, source_target_pairs={{0,4},{4,8},{8,12},{12,16},{16,20},{20,24},{24,28},{1,5},{5,9},{9,... | collective-permute-start | bytes 1572872 | tf_op jit(solution)/shard_map/ppermute | solution.py:17
  129.4 6.0 %collective-permute-done.1 = bf16[4,1,128,512]{3,2,1,0:T(8,128)(2,1)S(1)} collective-permute-done((bf16[4,1,128,512]{3,2,1,0:T(8,128)(2,1)S(1)}, bf16[4,1,128,512]{3,2,1,0:T(8,128)(2,1)S(1)}, u32[]{:S(2)}, u32[]{:S(2)}) %collective-permute-start.1) | collective-permute-done | bytes 524320 | tf_op jit(solution)/shard_map/ppermute | solution.py:17
  140.1 9.6 %fusion.35 = (bf16[1,1,3,512,512]{4,3,2,1,0:T(8,128)(2,1)}, bf16[1,1,3,512,512]{4,3,2,1,0:T(8,128)(2,1)}, bf16[1,1,3,512,512]{4,3,2,1,0:T(8,128)(2,1)}, bf16[1,1...) fusion(bf16[3,3,3,512,512]{4,3,2,1,0:T(8,128)(2,1)} %param.12), kind=kLoop, calls=%fused_computation.77 | loop fusion | bytes 28311552 | tf_op jit(solution)/shard_map/slice | solution.py:89
  149.8 9.9 %fusion.11 = bf16[4,10,130,512]{3,2,1,0:T(8,128)(2,1)} fusion(bf16[4,1,128,512]{3,2,1,0:T(8,128)(2,1)S(1)} %broadcast_select_fusion.3, bf16[4,1,128,512]{3,2,1,0:T(8,128)(2,1)S(1)} %get-tuple-element.18, bf16[2,8,128,512]{3,2,1,0:T(8,128)(2,1)S(1)} %fusion.24, bf16[2,8,128,512]{3,2,1,0:T(8,128)(2,1)} %collective-permute-done), kind=kLoop, calls=%fused_computation.29 | loop fusion | flops 90521600 | bytes 10567680 | tf_op jit(solution)/shard_map/jit(_pad)/concatenate | solution.py:129
  163.0 4.9 %gather_fusion.1 = bf16[2,10,130,512]{3,2,1,0:T(8,128)(2,1)} fusion(bf16[4,10,130,512]{3,2,1,0:T(8,128)(2,1)} %fusion.11, s32[1024]{0:T(1024)S(1)} %pad_clamp_fusion.1), kind=kCustom, calls=%fused_computation.1.clone | custom fusion | bytes 5324808 | tf_op jit(solution)/shard_map/jit(_take)/gather | solution.py:80
  168.0 4.9 %gather_fusion = bf16[2,10,130,512]{3,2,1,0:T(8,128)(2,1)} fusion(bf16[4,10,130,512]{3,2,1,0:T(8,128)(2,1)} %fusion.11, s32[1024]{0:T(1024)S(1)} %pad_clamp_fusion.2), kind=kCustom, calls=%fused_computation.clone | custom fusion | bytes 5324808 | tf_op jit(solution)/shard_map/jit(_take)/gather | solution.py:80
  175.2 8.0 %fusion.36 = (bf16[2,8,128,512]{3,2,1,0:T(8,128)(2,1)}, bf16[2,8,128,512]{3,2,1,0:T(8,128)(2,1)}, bf16[2,8,128,512]{3,2,1,0:T(8,128)(2,1)}, bf16[2,8,128,512]{3,...) fusion(bf16[2,10,130,512]{3,2,1,0:T(8,128)(2,1)S(1)} %get-tuple, ...), kind=kLoop, calls=%fused_computation.78 | loop fusion | bytes 37748736 | tf_op jit(solution)/shard_map/slice | solution.py:84
  183.5 6.8 %fusion.37 = (bf16[2,8,128,512]{3,2,1,0:T(8,128)(2,1)S(1)}, bf16[2,8,128,512]{3,2,1,0:T(8,128)(2,1)}, bf16[2,8,128,512]{3,2,1,0:T(8,128)(2,1)}, bf16[2,8,128,512...) fusion(bf16[2,10,130,512]{3,2,1,0:T(8,128)(2,1)S(1)} %broadcast, ...), kind=kLoop, calls=%fused_computation.79 | loop fusion | bytes 37748736 | tf_op jit(solution)/shard_map/slice | solution.py:84
  190.3 7.1 %fusion.38 = (bf16[2,8,128,512]{3,2,1,0:T(8,128)(2,1)}, bf16[2,8,128,512]{3,2,1,0:T(8,128)(2,1)}, bf16[2,8,128,512]{3,2,1,0:T(8,128)(2,1)}, bf16[2,8,128,512]{3,...) fusion(bf16[2,10,130,512]{3,2,1,0:T(8,128)(2,1)S(1)} %get-tuple, ...), kind=kLoop, calls=%fused_computation.80 | loop fusion | bytes 37748736 | tf_op jit(solution)/shard_map/slice | solution.py:84
  201.1 4.9 %fusion.48 = f32[2048,512]{1,0:T(8,128)} fusion(bf16[2048,1536]{1,0:T(8,128)(2,1)S(1)} %bitcast.49, bf16[1536,512]{1,0:T(8,128)(2,1)S(1)} %bitcast.64), kind=kOutput, calls=%fused_computation.90 | convolution fusion | flops 3221225472 | bytes 12058624 | tf_op jit(solution)/shard_map/dot_general | solution.py:90
  206.0 4.4 %pad_maximum_fusion.6 = bf16[2,8,128,1536]{3,2,1,0:T(8,128)(2,1)S(1)} fusion(bf16[2,8,128,512]{3,2,1,0:T(8,128)(2,1)S(1)} %copy-done.17, bf16[2,8,128,512]{3,2,1,0:T(8,128)(2,1)S(1)} %copy-done.18, bf16[2,8,128,512]{3,2,1,0:T(8,128)(2,1)S(1)} %copy-done.19), kind=kLoop, calls=%fused_computation.23 | loop fusion | flops 18874368 | bytes 12582912 | tf_op jit(solution)/shard_map/concatenate | solution.py:82
  210.5 4.9 %fusion.47 = f32[2048,512]{1,0:T(8,128)} fusion(bf16[2048,1536]{1,0:T(8,128)(2,1)S(1)} %bitcast.50, bf16[1536,512]{1,0:T(8,128)(2,1)S(1)} %bitcast.63), kind=kOutput, calls=%fused_computation.89 | convolution fusion | flops 3221225472 | bytes 12058624 | tf_op jit(solution)/shard_map/dot_general | solution.py:90
  216.8 4.9 %fusion.41 = f32[2048,512]{1,0:T(8,128)} fusion(bf16[2048,1536]{1,0:T(8,128)(2,1)S(1)} %bitcast.56, bf16[1536,512]{1,0:T(8,128)(2,1)S(1)} %bitcast.62), kind=kOutput, calls=%fused_computation.83 | convolution fusion | flops 3221225472 | bytes 12058624 | tf_op jit(solution)/shard_map/dot_general | solution.py:90
  221.7 4.9 %fusion.42 = f32[2048,512]{1,0:T(8,128)} fusion(bf16[2048,1536]{1,0:T(8,128)(2,1)S(1)} %bitcast.55, bf16[1536,512]{1,0:T(8,128)(2,1)S(1)} %bitcast.61), kind=kOutput, calls=%fused_computation.84 | convolution fusion | flops 3221225472 | bytes 12058624 | tf_op jit(solution)/shard_map/dot_general | solution.py:90
  230.9 4.9 %fusion.43 = f32[2048,512]{1,0:T(8,128)} fusion(bf16[2048,1536]{1,0:T(8,128)(2,1)S(1)} %bitcast.51, bf16[1536,512]{1,0:T(8,128)(2,1)S(1)} %bitcast.60), kind=kOutput, calls=%fused_computation.85 | convolution fusion | flops 3221225472 | bytes 12058624 | tf_op jit(solution)/shard_map/dot_general | solution.py:90
  235.8 4.2 %pad_maximum_fusion.3 = bf16[2,8,128,1536]{3,2,1,0:T(8,128)(2,1)S(1)} fusion(bf16[2,8,128,512]{3,2,1,0:T(8,128)(2,1)S(1)} %copy-done.12, bf16[2,8,128,512]{3,2,1,0:T(8,128)(2,1)S(1)} %copy-done.13, bf16[2,8,128,512]{3,2,1,0:T(8,128)(2,1)S(1)} %copy-done.11), kind=kLoop, calls=%fused_computation.20 | loop fusion | flops 18874368 | bytes 12582912 | tf_op jit(solution)/shard_map/concatenate | solution.py:82
  240.1 4.9 %fusion.44 = f32[2048,512]{1,0:T(8,128)} fusion(bf16[2048,1536]{1,0:T(8,128)(2,1)S(1)} %bitcast.52, bf16[1536,512]{1,0:T(8,128)(2,1)S(1)} %bitcast.59), kind=kOutput, calls=%fused_computation.86 | convolution fusion | flops 3221225472 | bytes 12058624 | tf_op jit(solution)/shard_map/dot_general | solution.py:90
  249.3 4.9 %fusion.46 = f32[2048,512]{1,0:T(8,128)} fusion(bf16[2048,1536]{1,0:T(8,128)(2,1)S(1)} %bitcast.53, bf16[1536,512]{1,0:T(8,128)(2,1)S(1)} %bitcast.58), kind=kOutput, calls=%fused_computation.88 | convolution fusion | flops 3221225472 | bytes 12058624 | tf_op jit(solution)/shard_map/dot_general | solution.py:90
  254.3 4.5 %pad_maximum_fusion.4 = bf16[2,8,128,1536]{3,2,1,0:T(8,128)(2,1)S(1)} fusion(bf16[2,8,128,512]{3,2,1,0:T(8,128)(2,1)S(1)} %get-tuple-element.51, bf16[2,8,128,512]{3,2,1,0:T(8,128)(2,1)S(1)} %copy-done.6, bf16[2,8,128,512]{3,2,1,0:T(8,128)(2,1)S(1)} %copy-done.7), kind=kLoop, calls=%fused_computation.21 | loop fusion | flops 18874368 | bytes 12582912 | tf_op jit(solution)/shard_map/concatenate | solution.py:82
  258.8 5.0 %fusion.45 = f32[2048,512]{1,0:T(8,128)} fusion(bf16[2048,1536]{1,0:T(8,128)(2,1)S(1)} %bitcast.54, bf16[1536,512]{1,0:T(8,128)(2,1)S(1)} %bitcast.57), kind=kOutput, calls=%fused_computation.87 | convolution fusion | flops 3221225472 | bytes 12058624 | tf_op jit(solution)/shard_map/dot_general | solution.py:90
  268.0 14.8 %add_add_fusion = f32[2048,512]{1,0:T(8,128)} fusion(f32[2048,512]{1,0:T(8,128)} %fusion.48, f32[2048,512]{1,0:T(8,128)} %fusion.47, f32[2048,512]{1,0:T(8,128)} %fusion.46, f32[2048,512]{1,0:T(8,128)} %fusion.45, f32[2048,512]{1,0:T(8,128)} %fusion.44, f32[2048,512]{1,0:T(8,128)} %fusion.43, f32[2048,512]{1,0:T(8,128)} %fusion.41, ...), kind=kOutput, calls=%fused_computation.46 | convolution fusion | flops 3229614080 | bytes 45613056 | tf_op jit(solution)/shard_map/dot_general | solution.py:90
  282.8 4.4 %fusion.27 = bf16[2,8,128,512]{3,2,1,0:T(8,128)(2,1)} fusion(f32[2,8,128,512]{3,2,1,0:T(8,128)} %bitcast.47, bf16[2,8,128,512]{3,2,1,0:T(8,128)(2,1)S(1)} %copy-done, f32[512]{0:T(512)S(1)} %copy-done.28), kind=kLoop, calls=%fused_computation.45 | loop fusion | flops 4194304 | bytes 8390656 | tf_op jit(solution)/shard_map/convert_element_type | solution.py:139
  (94 shorter events, 39.8 us)
Async XLA Ops:
  73.4 50.6 %collective-permute-start = (bf16[2,8,128,512]{3,2,1,0:T(8,128)(2,1)S(1)}, bf16[2,8,128,512]{3,2,1,0:T(8,128)(2,1)}, u32[]{:S(2)}, u32[]{:S(2)}) collective-permute-start(bf16[2,8,128,512]{3,2,1,0:T(8,128)(2,1)S(1)} %fusion.24), channel_id=1, source_target_pairs={{0,1},{1,2},{2,3},{3,32},{32,33},{33,34},{34,35},{35,64},{64,65},{... | collective-permute-start | bytes 6291464 | tf_op jit(solution)/shard_map/ppermute | solution.py:26
  124.9 10.5 %collective-permute-start.1 = (bf16[4,1,128,512]{3,2,1,0:T(8,128)(2,1)S(1)}, bf16[4,1,128,512]{3,2,1,0:T(8,128)(2,1)S(1)}, u32[]{:S(2)}, u32[]{:S(2)}) collective-permute-start(bf16[4,1,128,512]{3,2,1,0:T(8,128)(2,1)S(1)} %pad_maximum_fusion.9), channel_id=1, source_target_pairs={{0,4},{4,8},{8,12},{12,16},{16,20},{20,24},{24,28},{1,5},{5,9},{9,... | collective-permute-start | bytes 1572872 | tf_op jit(solution)/shard_map/ppermute | solution.py:17
  136.5 13.2 %collective-permute-start.2 = (bf16[4,1,128,512]{3,2,1,0:T(8,128)(2,1)S(1)}, bf16[4,1,128,512]{3,2,1,0:T(8,128)(2,1)S(1)}, u32[]{:S(2)}, u32[]{:S(2)}) collective-permute-start(bf16[4,1,128,512]{3,2,1,0:T(8,128)(2,1)S(1)} %get-tuple-element.19), channel_id=1, source_target_pairs={{4,0},{8,4},{12,8},{16,12},{20,16},{24,20},{28,24},{5,1},{9,5},{13... | collective-permute-start | bytes 1572872 | tf_op jit(solution)/shard_map/ppermute | solution.py:18
  175.2 8.0 %copy-start.1 = (bf16[2,10,130,512]{3,2,1,0:T(8,128)(2,1)S(1)}, bf16[2,10,130,512]{3,2,1,0:T(8,128)(2,1)}, u32[]{:S(2)}) copy-start(bf16[2,10,130,512]{3,2,1,0:T(8,128)(2,1)} %gather_fusion) | copy-start | bytes 7987204
  201.1 4.9 %copy-start.17 = (bf16[2,8,128,512]{3,2,1,0:T(8,128)(2,1)S(1)}, bf16[2,8,128,512]{3,2,1,0:T(8,128)(2,1)}, u32[]{:S(2)}) copy-start(bf16[2,8,128,512]{3,2,1,0:T(8,128)(2,1)} %get-tuple-element.35) | copy-start | bytes 6291460
  201.1 4.9 %copy-start.18 = (bf16[2,8,128,512]{3,2,1,0:T(8,128)(2,1)S(1)}, bf16[2,8,128,512]{3,2,1,0:T(8,128)(2,1)}, u32[]{:S(2)}) copy-start(bf16[2,8,128,512]{3,2,1,0:T(8,128)(2,1)} %get-tuple-element.36) | copy-start | bytes 6291460
  201.1 4.9 %copy-start.19 = (bf16[2,8,128,512]{3,2,1,0:T(8,128)(2,1)S(1)}, bf16[2,8,128,512]{3,2,1,0:T(8,128)(2,1)}, u32[]{:S(2)}) copy-start(bf16[2,8,128,512]{3,2,1,0:T(8,128)(2,1)} %get-tuple-element.37) | copy-start | bytes 6291460
  210.5 4.9 %copy-start.2 = (bf16[2,8,128,512]{3,2,1,0:T(8,128)(2,1)S(1)}, bf16[2,8,128,512]{3,2,1,0:T(8,128)(2,1)}, u32[]{:S(2)}) copy-start(bf16[2,8,128,512]{3,2,1,0:T(8,128)(2,1)} %get-tuple-element.46) | copy-start | bytes 6291460
  221.7 4.9 %copy-start.14 = (bf16[2,8,128,512]{3,2,1,0:T(8,128)(2,1)S(1)}, bf16[2,8,128,512]{3,2,1,0:T(8,128)(2,1)}, u32[]{:S(2)}) copy-start(bf16[2,8,128,512]{3,2,1,0:T(8,128)(2,1)} %get-tuple-element.39) | copy-start | bytes 6291460
  221.7 4.9 %copy-start.15 = (bf16[2,8,128,512]{3,2,1,0:T(8,128)(2,1)S(1)}, bf16[2,8,128,512]{3,2,1,0:T(8,128)(2,1)}, u32[]{:S(2)}) copy-start(bf16[2,8,128,512]{3,2,1,0:T(8,128)(2,1)} %get-tuple-element.40) | copy-start | bytes 6291460
  221.7 4.9 %copy-start.16 = (bf16[2,8,128,512]{3,2,1,0:T(8,128)(2,1)S(1)}, bf16[2,8,128,512]{3,2,1,0:T(8,128)(2,1)}, u32[]{:S(2)}) copy-start(bf16[2,8,128,512]{3,2,1,0:T(8,128)(2,1)} %get-tuple-element.41) | copy-start | bytes 6291460
  230.9 4.9 %copy-start.11 = (bf16[2,8,128,512]{3,2,1,0:T(8,128)(2,1)S(1)}, bf16[2,8,128,512]{3,2,1,0:T(8,128)(2,1)}, u32[]{:S(2)}) copy-start(bf16[2,8,128,512]{3,2,1,0:T(8,128)(2,1)} %get-tuple-element.47) | copy-start | bytes 6291460
  230.9 4.9 %copy-start.12 = (bf16[2,8,128,512]{3,2,1,0:T(8,128)(2,1)S(1)}, bf16[2,8,128,512]{3,2,1,0:T(8,128)(2,1)}, u32[]{:S(2)}) copy-start(bf16[2,8,128,512]{3,2,1,0:T(8,128)(2,1)} %get-tuple-element.54) | copy-start | bytes 6291460
  230.9 4.9 %copy-start.13 = (bf16[2,8,128,512]{3,2,1,0:T(8,128)(2,1)S(1)}, bf16[2,8,128,512]{3,2,1,0:T(8,128)(2,1)}, u32[]{:S(2)}) copy-start(bf16[2,8,128,512]{3,2,1,0:T(8,128)(2,1)} %get-tuple-element.55) | copy-start | bytes 6291460
  240.1 5.0 %copy-start.8 = (bf16[2,8,128,512]{3,2,1,0:T(8,128)(2,1)S(1)}, bf16[2,8,128,512]{3,2,1,0:T(8,128)(2,1)}, u32[]{:S(2)}) copy-start(bf16[2,8,128,512]{3,2,1,0:T(8,128)(2,1)} %get-tuple-element.48) | copy-start | bytes 6291460
  240.1 5.0 %copy-start.9 = (bf16[2,8,128,512]{3,2,1,0:T(8,128)(2,1)S(1)}, bf16[2,8,128,512]{3,2,1,0:T(8,128)(2,1)}, u32[]{:S(2)}) copy-start(bf16[2,8,128,512]{3,2,1,0:T(8,128)(2,1)} %get-tuple-element.49) | copy-start | bytes 6291460
  240.1 5.0 %copy-start.10 = (bf16[2,8,128,512]{3,2,1,0:T(8,128)(2,1)S(1)}, bf16[2,8,128,512]{3,2,1,0:T(8,128)(2,1)}, u32[]{:S(2)}) copy-start(bf16[2,8,128,512]{3,2,1,0:T(8,128)(2,1)} %get-tuple-element.50) | copy-start | bytes 6291460
  249.3 5.0 %copy-start.6 = (bf16[2,8,128,512]{3,2,1,0:T(8,128)(2,1)S(1)}, bf16[2,8,128,512]{3,2,1,0:T(8,128)(2,1)}, u32[]{:S(2)}) copy-start(bf16[2,8,128,512]{3,2,1,0:T(8,128)(2,1)} %get-tuple-element.52) | copy-start | bytes 6291460
  249.3 4.9 %copy-start.7 = (bf16[2,8,128,512]{3,2,1,0:T(8,128)(2,1)S(1)}, bf16[2,8,128,512]{3,2,1,0:T(8,128)(2,1)}, u32[]{:S(2)}) copy-start(bf16[2,8,128,512]{3,2,1,0:T(8,128)(2,1)} %get-tuple-element.53) | copy-start | bytes 6291460
  258.8 5.0 %copy-start.3 = (bf16[2,8,128,512]{3,2,1,0:T(8,128)(2,1)S(1)}, bf16[2,8,128,512]{3,2,1,0:T(8,128)(2,1)}, u32[]{:S(2)}) copy-start(bf16[2,8,128,512]{3,2,1,0:T(8,128)(2,1)} %get-tuple-element.29) | copy-start | bytes 6291460
  258.8 5.0 %copy-start.4 = (bf16[2,8,128,512]{3,2,1,0:T(8,128)(2,1)S(1)}, bf16[2,8,128,512]{3,2,1,0:T(8,128)(2,1)}, u32[]{:S(2)}) copy-start(bf16[2,8,128,512]{3,2,1,0:T(8,128)(2,1)} %get-tuple-element.30) | copy-start | bytes 6291460
  258.8 5.0 %copy-start.5 = (bf16[2,8,128,512]{3,2,1,0:T(8,128)(2,1)S(1)}, bf16[2,8,128,512]{3,2,1,0:T(8,128)(2,1)}, u32[]{:S(2)}) copy-start(bf16[2,8,128,512]{3,2,1,0:T(8,128)(2,1)} %get-tuple-element.31) | copy-start | bytes 6291460
  268.0 14.8 %copy-start = (bf16[2,8,128,512]{3,2,1,0:T(8,128)(2,1)S(1)}, bf16[2,8,128,512]{3,2,1,0:T(8,128)(2,1)}, u32[]{:S(2)}) copy-start(bf16[2,8,128,512]{3,2,1,0:T(8,128)(2,1)} %param.8) | copy-start | bytes 6291460
  268.0 14.8 %copy-start.28 = (f32[512]{0:T(512)S(1)}, f32[512]{0:T(512)}, u32[]{:S(2)}) copy-start(f32[512]{0:T(512)} %param.13) | copy-start | bytes 6148
  (8 other events, 31.7 us)
where the time goes:
time: 288 us; the launch traced here: 287 us
  blocking collectives  65 us (23%)
  other arithmetic  56.8 us (20%)
  matrix products  54.9 us (19%)
  waiting for transfers between devices  54.7 us (19%)
  local copies, waits for them, and re-layouts  45.4 us (16%)
  starting transfers between devices  10 us (3%)
    psum x1, blocking collectives, finish_stats(): lax.psum((local_sums, local_squares), ('req', 'tile', 'span'))  65 us
    dot_general x9, matrix products, convolve(): jnp.dot(stacked.reshape(frame_count * row_count * col_count, 3 * channels...  54.1 us
    ppermute x1, waiting for transfers between devices, shifted(): return lax.ppermute(array, axis, pairs)  48.6 us
    concatenate x8, other arithmetic, convolve(): jnp.concatenate([chosen[:, row_tap:row_tap + row_count, col_tap:col_tap +...  30.7 us
    slice x3, local copies, waits for them, and re-layouts, convolve(): chosen[:, row_tap:row_tap + row_count, col_tap:col_tap + col_count]  21.8 us
    gather x3, local copies, waits for them, and re-layouts, convolve(): chosen = jnp.take(padded, tap_index[time_tap], axis=0)  13.1 us
    concatenate x1, other arithmetic, shards(): padded = jnp.pad(extended, ((0, 0), (0, 0), (1, 1), (0, 0)), mode='edge')  9.92 us
    slice x1, local copies, waits for them, and re-layouts, convolve(): kernel = conv_weight[time_tap, row_tap].reshape(3 * channels, channels)  9.58 us
  transfers between devices with their start and end apart: 3, of which 2 were waited for; matrix products, arithmetic and copies ran while one was open for 3% of the time, Pallas kernels for 0%

commit v1 on v0

--- a/solution.py
+++ b/solution.py
@@ -1,10 +1,21 @@
+import functools
 import jax
 import jax.numpy as jnp
 from jax import lax
 from jax.sharding import PartitionSpec as P
+from jax.lax import psum
 
 GROUPS = 32
 EPSILON = 1e-06
+
+
+def ways_lead(inp, peer_axis, device_axis):
+    r2 = psum(inp, peer_axis)
+    current_block = psum(r2, device_axis)
+    return current_block
+
+
+store_the_forms = functools.partial(ways_lead, peer_axis=("tile", "span"), device_axis="req")
 
 
 def extended_2(array, sides, width):
@@ -50,7 +61,7 @@
 
 
 def finish_stats(local_sums, local_squares, cell_count):
-    total_sums, total_squares = lax.psum((local_sums, local_squares), ("req", "tile", "span"))
+    total_sums, total_squares = store_the_forms((local_sums, local_squares))
     group_mean = total_sums / cell_count
     group_scale = lax.rsqrt(total_squares / cell_count - group_mean * group_mean + EPSILON)
     return (group_mean, group_scale)

time: 288 us -> 287 us (level); the launches traced: 287 us -> 283 us
  blocking collectives: 65 us -> 60.2 us
  starting transfers between devices: 10 us -> 13.8 us
  waiting for transfers between devices: 54.7 us -> 51.7 us
    psum x1 -> x2, blocking collectives: 65 us -> 60.2 us  [the longest x1 53.2 us: ways_lead(): r2 = psum(inp, peer_axis)]
    ppermute x1, starting transfers between devices: 4.42 us -> 8.15 us  [extended_2(): before = lax.ppermute(last, axis, up)]
    ppermute x1, waiting for transfers between devices: 48.6 us -> 45.6 us  [shifted(): return lax.ppermute(array, axis, pairs)]
where the time goes in v1:
time: 287 us; the launch traced here: 283 us
  blocking collectives  60.2 us (21%)
  other arithmetic  56.8 us (20%)
  matrix products  54.8 us (19%)
  waiting for transfers between devices  51.7 us (18%)
  local copies, waits for them, and re-layouts  45.4 us (16%)
  starting transfers between devices  13.8 us (5%)
    dot_general x9, matrix products, convolve(): jnp.dot(stacked.reshape(frame_count * row_count * col_count, 3 * channels...  54.1 us
    psum x1, blocking collectives, ways_lead(): r2 = psum(inp, peer_axis)  53.2 us
    ppermute x1, waiting for transfers between devices, shifted(): return lax.ppermute(array, axis, pairs)  45.6 us
    concatenate x8, other arithmetic, convolve(): jnp.concatenate([chosen[:, row_tap:row_tap + row_count, col_tap:col_tap +...  30.7 us
    slice x3, local copies, waits for them, and re-layouts, convolve(): chosen[:, row_tap:row_tap + row_count, col_tap:col_tap + col_count]  21.8 us
    gather x3, local copies, waits for them, and re-layouts, convolve(): chosen = jnp.take(padded, tap_index[time_tap], axis=0)  13.1 us
    concatenate x1, other arithmetic, shards(): padded = jnp.pad(extended, ((0, 0), (0, 0), (1, 1), (0, 0)), mode='edge')  9.91 us
    slice x1, local copies, waits for them, and re-layouts, convolve(): kernel = conv_weight[time_tap, row_tap].reshape(3 * channels, channels)  9.56 us
  transfers between devices with their start and end apart: 3, of which 2 were waited for; matrix products, arithmetic and copies ran while one was open for 3% of the time, Pallas kernels for 0%

profile of v1, /device:TPU:41, one launch (start us, length us, event | category | flops | bytes accessed | tf_op | source)
XLA Modules:
  0.0 283.1 jit_solution(17280928781474107687)
XLA Ops:
  4.6 53.2 %all-reduce = (f32[4,32]{1,0:T(4,128)S(1)}, f32[4,32]{1,0:T(4,128)S(1)}) all-reduce(f32[4,32]{1,0:T(4,128)S(1)} %fusion.40, f32[4,32]{1,0:T(4,128)S(1)} %fusion.39), channel_id=1, replica_groups=mesh['req'=4,'tile'=8,'span'=4] {'tile','span'}, use_global_device_ids=true, to_apply=%region_7.8 | all-reduce | flops 256 | bytes 2048 | tf_op jit(solution)/shard_map/psum | solution.py:13
  57.7 7.0 %all-reduce.1 = (f32[4,32]{1,0:T(4,128)S(1)}, f32[4,32]{1,0:T(4,128)S(1)}) all-reduce(f32[4,32]{1,0:T(4,128)S(1)} %get-tuple-element.8, f32[4,32]{1,0:T(4,128)S(1)} %get-tuple-element.9), channel_id=1, replica_groups=mesh['req'=4,'tile'=8,'span'=4] {'req'}, use_global_device_ids=true, to_apply=%region_8.9 | all-reduce | flops 256 | bytes 2048 | tf_op jit(solution)/shard_map/psum | solution.py:14
  70.5 45.6 %collective-permute-done = bf16[2,8,128,512]{3,2,1,0:T(8,128)(2,1)} collective-permute-done((bf16[2,8,128,512]{3,2,1,0:T(8,128)(2,1)S(1)}, bf16[2,8,128,512]{3,2,1,0:T(8,128)(2,1)}, u32[]{:S(2)}, u32[]{:S(2)}) %collective-permute-start) | collective-permute-done | bytes 2097184 | tf_op jit(solution)/shard_map/ppermute | solution.py:37
  117.1 8.1 %collective-permute-start.1 = (bf16[4,1,128,512]{3,2,1,0:T(8,128)(2,1)S(1)}, bf16[4,1,128,512]{3,2,1,0:T(8,128)(2,1)S(1)}, u32[]{:S(2)}, u32[]{:S(2)}) collective-permute-start(bf16[4,1,128,512]{3,2,1,0:T(8,128)(2,1)S(1)} %pad_maximum_fusion.9), channel_id=1, source_target_pairs={{0,4},{4,8},{8,12},{12,16},{16,20},{20,24},{24,28},{1,5},{5,9},{9,... | collective-permute-start | bytes 1572872 | tf_op jit(solution)/shard_map/ppermute | solution.py:28
  125.3 6.0 %collective-permute-done.1 = bf16[4,1,128,512]{3,2,1,0:T(8,128)(2,1)S(1)} collective-permute-done((bf16[4,1,128,512]{3,2,1,0:T(8,128)(2,1)S(1)}, bf16[4,1,128,512]{3,2,1,0:T(8,128)(2,1)S(1)}, u32[]{:S(2)}, u32[]{:S(2)}) %collective-permute-start.1) | collective-permute-done | bytes 524320 | tf_op jit(solution)/shard_map/ppermute | solution.py:28
  136.1 9.6 %fusion.35 = (bf16[1,1,3,512,512]{4,3,2,1,0:T(8,128)(2,1)}, bf16[1,1,3,512,512]{4,3,2,1,0:T(8,128)(2,1)}, bf16[1,1,3,512,512]{4,3,2,1,0:T(8,128)(2,1)}, bf16[1,1...) fusion(bf16[3,3,3,512,512]{4,3,2,1,0:T(8,128)(2,1)} %param.12), kind=kLoop, calls=%fused_computation.77 | loop fusion | bytes 28311552 | tf_op jit(solution)/shard_map/slice | solution.py:100
  145.7 9.9 %fusion.11 = bf16[4,10,130,512]{3,2,1,0:T(8,128)(2,1)} fusion(bf16[4,1,128,512]{3,2,1,0:T(8,128)(2,1)S(1)} %broadcast_select_fusion.3, bf16[4,1,128,512]{3,2,1,0:T(8,128)(2,1)S(1)} %get-tuple-element.20, bf16[2,8,128,512]{3,2,1,0:T(8,128)(2,1)S(1)} %fusion.24, bf16[2,8,128,512]{3,2,1,0:T(8,128)(2,1)} %collective-permute-done), kind=kLoop, calls=%fused_computation.29 | loop fusion | flops 90521600 | bytes 10567680 | tf_op jit(solution)/shard_map/jit(_pad)/concatenate | solution.py:140
  159.0 4.9 %gather_fusion.1 = bf16[2,10,130,512]{3,2,1,0:T(8,128)(2,1)} fusion(bf16[4,10,130,512]{3,2,1,0:T(8,128)(2,1)} %fusion.11, s32[1024]{0:T(1024)S(1)} %pad_clamp_fusion.1), kind=kCustom, calls=%fused_computation.1.clone | custom fusion | bytes 5324808 | tf_op jit(solution)/shard_map/jit(_take)/gather | solution.py:91
  163.9 4.9 %gather_fusion = bf16[2,10,130,512]{3,2,1,0:T(8,128)(2,1)} fusion(bf16[4,10,130,512]{3,2,1,0:T(8,128)(2,1)} %fusion.11, s32[1024]{0:T(1024)S(1)} %pad_clamp_fusion.2), kind=kCustom, calls=%fused_computation.clone | custom fusion | bytes 5324808 | tf_op jit(solution)/shard_map/jit(_take)/gather | solution.py:91
  171.1 8.0 %fusion.36 = (bf16[2,8,128,512]{3,2,1,0:T(8,128)(2,1)}, bf16[2,8,128,512]{3,2,1,0:T(8,128)(2,1)}, bf16[2,8,128,512]{3,2,1,0:T(8,128)(2,1)}, bf16[2,8,128,512]{3,...) fusion(bf16[2,10,130,512]{3,2,1,0:T(8,128)(2,1)S(1)} %get-tuple, ...), kind=kLoop, calls=%fused_computation.78 | loop fusion | bytes 37748736 | tf_op jit(solution)/shard_map/slice | solution.py:95
  179.4 6.8 %fusion.37 = (bf16[2,8,128,512]{3,2,1,0:T(8,128)(2,1)S(1)}, bf16[2,8,128,512]{3,2,1,0:T(8,128)(2,1)}, bf16[2,8,128,512]{3,2,1,0:T(8,128)(2,1)}, bf16[2,8,128,512...) fusion(bf16[2,10,130,512]{3,2,1,0:T(8,128)(2,1)S(1)} %broadcast, ...), kind=kLoop, calls=%fused_computation.79 | loop fusion | bytes 37748736 | tf_op jit(solution)/shard_map/slice | solution.py:95
  186.2 7.1 %fusion.38 = (bf16[2,8,128,512]{3,2,1,0:T(8,128)(2,1)}, bf16[2,8,128,512]{3,2,1,0:T(8,128)(2,1)}, bf16[2,8,128,512]{3,2,1,0:T(8,128)(2,1)}, bf16[2,8,128,512]{3,...) fusion(bf16[2,10,130,512]{3,2,1,0:T(8,128)(2,1)S(1)} %get-tuple, ...), kind=kLoop, calls=%fused_computation.80 | loop fusion | bytes 37748736 | tf_op jit(solution)/shard_map/slice | solution.py:95
  197.0 4.9 %fusion.48 = f32[2048,512]{1,0:T(8,128)} fusion(bf16[2048,1536]{1,0:T(8,128)(2,1)S(1)} %bitcast.49, bf16[1536,512]{1,0:T(8,128)(2,1)S(1)} %bitcast.64), kind=kOutput, calls=%fused_computation.90 | convolution fusion | flops 3221225472 | bytes 12058624 | tf_op jit(solution)/shard_map/dot_general | solution.py:101
  201.9 4.4 %pad_maximum_fusion.6 = bf16[2,8,128,1536]{3,2,1,0:T(8,128)(2,1)S(1)} fusion(bf16[2,8,128,512]{3,2,1,0:T(8,128)(2,1)S(1)} %copy-done.17, bf16[2,8,128,512]{3,2,1,0:T(8,128)(2,1)S(1)} %copy-done.18, bf16[2,8,128,512]{3,2,1,0:T(8,128)(2,1)S(1)} %copy-done.19), kind=kLoop, calls=%fused_computation.23 | loop fusion | flops 18874368 | bytes 12582912 | tf_op jit(solution)/shard_map/concatenate | solution.py:93
  206.4 4.9 %fusion.47 = f32[2048,512]{1,0:T(8,128)} fusion(bf16[2048,1536]{1,0:T(8,128)(2,1)S(1)} %bitcast.50, bf16[1536,512]{1,0:T(8,128)(2,1)S(1)} %bitcast.63), kind=kOutput, calls=%fused_computation.89 | convolution fusion | flops 3221225472 | bytes 12058624 | tf_op jit(solution)/shard_map/dot_general | solution.py:101
  212.7 4.9 %fusion.41 = f32[2048,512]{1,0:T(8,128)} fusion(bf16[2048,1536]{1,0:T(8,128)(2,1)S(1)} %bitcast.56, bf16[1536,512]{1,0:T(8,128)(2,1)S(1)} %bitcast.62), kind=kOutput, calls=%fused_computation.83 | convolution fusion | flops 3221225472 | bytes 12058624 | tf_op jit(solution)/shard_map/dot_general | solution.py:101
  217.6 4.9 %fusion.42 = f32[2048,512]{1,0:T(8,128)} fusion(bf16[2048,1536]{1,0:T(8,128)(2,1)S(1)} %bitcast.55, bf16[1536,512]{1,0:T(8,128)(2,1)S(1)} %bitcast.61), kind=kOutput, calls=%fused_computation.84 | convolution fusion | flops 3221225472 | bytes 12058624 | tf_op jit(solution)/shard_map/dot_general | solution.py:101
  226.8 4.9 %fusion.43 = f32[2048,512]{1,0:T(8,128)} fusion(bf16[2048,1536]{1,0:T(8,128)(2,1)S(1)} %bitcast.51, bf16[1536,512]{1,0:T(8,128)(2,1)S(1)} %bitcast.60), kind=kOutput, calls=%fused_computation.85 | convolution fusion | flops 3221225472 | bytes 12058624 | tf_op jit(solution)/shard_map/dot_general | solution.py:101
  236.0 5.0 %fusion.44 = f32[2048,512]{1,0:T(8,128)} fusion(bf16[2048,1536]{1,0:T(8,128)(2,1)S(1)} %bitcast.52, bf16[1536,512]{1,0:T(8,128)(2,1)S(1)} %bitcast.59), kind=kOutput, calls=%fused_computation.86 | convolution fusion | flops 3221225472 | bytes 12058624 | tf_op jit(solution)/shard_map/dot_general | solution.py:101
  245.2 4.9 %fusion.46 = f32[2048,512]{1,0:T(8,128)} fusion(bf16[2048,1536]{1,0:T(8,128)(2,1)S(1)} %bitcast.53, bf16[1536,512]{1,0:T(8,128)(2,1)S(1)} %bitcast.58), kind=kOutput, calls=%fused_computation.88 | convolution fusion | flops 3221225472 | bytes 12058624 | tf_op jit(solution)/shard_map/dot_general | solution.py:101
  250.2 4.5 %pad_maximum_fusion.4 = bf16[2,8,128,1536]{3,2,1,0:T(8,128)(2,1)S(1)} fusion(bf16[2,8,128,512]{3,2,1,0:T(8,128)(2,1)S(1)} %get-tuple-element.53, bf16[2,8,128,512]{3,2,1,0:T(8,128)(2,1)S(1)} %copy-done.6, bf16[2,8,128,512]{3,2,1,0:T(8,128)(2,1)S(1)} %copy-done.7), kind=kLoop, calls=%fused_computation.21 | loop fusion | flops 18874368 | bytes 12582912 | tf_op jit(solution)/shard_map/concatenate | solution.py:93
  254.7 5.0 %fusion.45 = f32[2048,512]{1,0:T(8,128)} fusion(bf16[2048,1536]{1,0:T(8,128)(2,1)S(1)} %bitcast.54, bf16[1536,512]{1,0:T(8,128)(2,1)S(1)} %bitcast.57), kind=kOutput, calls=%fused_computation.87 | convolution fusion | flops 3221225472 | bytes 12058624 | tf_op jit(solution)/shard_map/dot_general | solution.py:101
  263.9 14.8 %add_add_fusion = f32[2048,512]{1,0:T(8,128)} fusion(f32[2048,512]{1,0:T(8,128)} %fusion.48, f32[2048,512]{1,0:T(8,128)} %fusion.47, f32[2048,512]{1,0:T(8,128)} %fusion.46, f32[2048,512]{1,0:T(8,128)} %fusion.45, f32[2048,512]{1,0:T(8,128)} %fusion.44, f32[2048,512]{1,0:T(8,128)} %fusion.43, f32[2048,512]{1,0:T(8,128)} %fusion.41, ...), kind=kOutput, calls=%fused_computation.46 | convolution fusion | flops 3229614080 | bytes 45613056 | tf_op jit(solution)/shard_map/dot_general | solution.py:101
  278.7 4.4 %fusion.27 = bf16[2,8,128,512]{3,2,1,0:T(8,128)(2,1)} fusion(f32[2,8,128,512]{3,2,1,0:T(8,128)} %bitcast.47, bf16[2,8,128,512]{3,2,1,0:T(8,128)(2,1)S(1)} %copy-done, f32[512]{0:T(512)S(1)} %copy-done.28), kind=kLoop, calls=%fused_computation.45 | loop fusion | flops 4194304 | bytes 8390656 | tf_op jit(solution)/shard_map/convert_element_type | solution.py:150
  (95 shorter events, 44.1 us)
Async XLA Ops:
  68.5 47.6 %collective-permute-start = (bf16[2,8,128,512]{3,2,1,0:T(8,128)(2,1)S(1)}, bf16[2,8,128,512]{3,2,1,0:T(8,128)(2,1)}, u32[]{:S(2)}, u32[]{:S(2)}) collective-permute-start(bf16[2,8,128,512]{3,2,1,0:T(8,128)(2,1)S(1)} %fusion.24), channel_id=1, source_target_pairs={{0,1},{1,2},{2,3},{3,32},{32,33},{33,34},{34,35},{35,64},{64,65},{... | collective-permute-start | bytes 6291464 | tf_op jit(solution)/shard_map/ppermute | solution.py:37
  117.1 14.3 %collective-permute-start.1 = (bf16[4,1,128,512]{3,2,1,0:T(8,128)(2,1)S(1)}, bf16[4,1,128,512]{3,2,1,0:T(8,128)(2,1)S(1)}, u32[]{:S(2)}, u32[]{:S(2)}) collective-permute-start(bf16[4,1,128,512]{3,2,1,0:T(8,128)(2,1)S(1)} %pad_maximum_fusion.9), channel_id=1, source_target_pairs={{0,4},{4,8},{8,12},{12,16},{16,20},{20,24},{24,28},{1,5},{5,9},{9,... | collective-permute-start | bytes 1572872 | tf_op jit(solution)/shard_map/ppermute | solution.py:28
  132.4 13.3 %collective-permute-start.2 = (bf16[4,1,128,512]{3,2,1,0:T(8,128)(2,1)S(1)}, bf16[4,1,128,512]{3,2,1,0:T(8,128)(2,1)S(1)}, u32[]{:S(2)}, u32[]{:S(2)}) collective-permute-start(bf16[4,1,128,512]{3,2,1,0:T(8,128)(2,1)S(1)} %get-tuple-element.21), channel_id=1, source_target_pairs={{4,0},{8,4},{12,8},{16,12},{20,16},{24,20},{28,24},{5,1},{9,5},{13... | collective-permute-start | bytes 1572872 | tf_op jit(solution)/shard_map/ppermute | solution.py:29
  171.1 8.0 %copy-start.1 = (bf16[2,10,130,512]{3,2,1,0:T(8,128)(2,1)S(1)}, bf16[2,10,130,512]{3,2,1,0:T(8,128)(2,1)}, u32[]{:S(2)}) copy-start(bf16[2,10,130,512]{3,2,1,0:T(8,128)(2,1)} %gather_fusion) | copy-start | bytes 7987204
  197.0 4.9 %copy-start.17 = (bf16[2,8,128,512]{3,2,1,0:T(8,128)(2,1)S(1)}, bf16[2,8,128,512]{3,2,1,0:T(8,128)(2,1)}, u32[]{:S(2)}) copy-start(bf16[2,8,128,512]{3,2,1,0:T(8,128)(2,1)} %get-tuple-element.37) | copy-start | bytes 6291460
  197.0 4.9 %copy-start.18 = (bf16[2,8,128,512]{3,2,1,0:T(8,128)(2,1)S(1)}, bf16[2,8,128,512]{3,2,1,0:T(8,128)(2,1)}, u32[]{:S(2)}) copy-start(bf16[2,8,128,512]{3,2,1,0:T(8,128)(2,1)} %get-tuple-element.38) | copy-start | bytes 6291460
  197.0 4.9 %copy-start.19 = (bf16[2,8,128,512]{3,2,1,0:T(8,128)(2,1)S(1)}, bf16[2,8,128,512]{3,2,1,0:T(8,128)(2,1)}, u32[]{:S(2)}) copy-start(bf16[2,8,128,512]{3,2,1,0:T(8,128)(2,1)} %get-tuple-element.39) | copy-start | bytes 6291460
  206.4 4.9 %copy-start.2 = (bf16[2,8,128,512]{3,2,1,0:T(8,128)(2,1)S(1)}, bf16[2,8,128,512]{3,2,1,0:T(8,128)(2,1)}, u32[]{:S(2)}) copy-start(bf16[2,8,128,512]{3,2,1,0:T(8,128)(2,1)} %get-tuple-element.48) | copy-start | bytes 6291460
  217.6 4.9 %copy-start.14 = (bf16[2,8,128,512]{3,2,1,0:T(8,128)(2,1)S(1)}, bf16[2,8,128,512]{3,2,1,0:T(8,128)(2,1)}, u32[]{:S(2)}) copy-start(bf16[2,8,128,512]{3,2,1,0:T(8,128)(2,1)} %get-tuple-element.41) | copy-start | bytes 6291460
  217.6 4.9 %copy-start.15 = (bf16[2,8,128,512]{3,2,1,0:T(8,128)(2,1)S(1)}, bf16[2,8,128,512]{3,2,1,0:T(8,128)(2,1)}, u32[]{:S(2)}) copy-start(bf16[2,8,128,512]{3,2,1,0:T(8,128)(2,1)} %get-tuple-element.42) | copy-start | bytes 6291460
  217.6 4.9 %copy-start.16 = (bf16[2,8,128,512]{3,2,1,0:T(8,128)(2,1)S(1)}, bf16[2,8,128,512]{3,2,1,0:T(8,128)(2,1)}, u32[]{:S(2)}) copy-start(bf16[2,8,128,512]{3,2,1,0:T(8,128)(2,1)} %get-tuple-element.43) | copy-start | bytes 6291460
  226.8 4.9 %copy-start.11 = (bf16[2,8,128,512]{3,2,1,0:T(8,128)(2,1)S(1)}, bf16[2,8,128,512]{3,2,1,0:T(8,128)(2,1)}, u32[]{:S(2)}) copy-start(bf16[2,8,128,512]{3,2,1,0:T(8,128)(2,1)} %get-tuple-element.49) | copy-start | bytes 6291460
  226.8 4.9 %copy-start.12 = (bf16[2,8,128,512]{3,2,1,0:T(8,128)(2,1)S(1)}, bf16[2,8,128,512]{3,2,1,0:T(8,128)(2,1)}, u32[]{:S(2)}) copy-start(bf16[2,8,128,512]{3,2,1,0:T(8,128)(2,1)} %get-tuple-element.56) | copy-start | bytes 6291460
  226.8 4.9 %copy-start.13 = (bf16[2,8,128,512]{3,2,1,0:T(8,128)(2,1)S(1)}, bf16[2,8,128,512]{3,2,1,0:T(8,128)(2,1)}, u32[]{:S(2)}) copy-start(bf16[2,8,128,512]{3,2,1,0:T(8,128)(2,1)} %get-tuple-element.57) | copy-start | bytes 6291460
  236.0 5.0 %copy-start.8 = (bf16[2,8,128,512]{3,2,1,0:T(8,128)(2,1)S(1)}, bf16[2,8,128,512]{3,2,1,0:T(8,128)(2,1)}, u32[]{:S(2)}) copy-start(bf16[2,8,128,512]{3,2,1,0:T(8,128)(2,1)} %get-tuple-element.50) | copy-start | bytes 6291460
  236.0 5.0 %copy-start.9 = (bf16[2,8,128,512]{3,2,1,0:T(8,128)(2,1)S(1)}, bf16[2,8,128,512]{3,2,1,0:T(8,128)(2,1)}, u32[]{:S(2)}) copy-start(bf16[2,8,128,512]{3,2,1,0:T(8,128)(2,1)} %get-tuple-element.51) | copy-start | bytes 6291460
  236.0 5.0 %copy-start.10 = (bf16[2,8,128,512]{3,2,1,0:T(8,128)(2,1)S(1)}, bf16[2,8,128,512]{3,2,1,0:T(8,128)(2,1)}, u32[]{:S(2)}) copy-start(bf16[2,8,128,512]{3,2,1,0:T(8,128)(2,1)} %get-tuple-element.52) | copy-start | bytes 6291460
  245.2 5.0 %copy-start.6 = (bf16[2,8,128,512]{3,2,1,0:T(8,128)(2,1)S(1)}, bf16[2,8,128,512]{3,2,1,0:T(8,128)(2,1)}, u32[]{:S(2)}) copy-start(bf16[2,8,128,512]{3,2,1,0:T(8,128)(2,1)} %get-tuple-element.54) | copy-start | bytes 6291460
  245.2 4.9 %copy-start.7 = (bf16[2,8,128,512]{3,2,1,0:T(8,128)(2,1)S(1)}, bf16[2,8,128,512]{3,2,1,0:T(8,128)(2,1)}, u32[]{:S(2)}) copy-start(bf16[2,8,128,512]{3,2,1,0:T(8,128)(2,1)} %get-tuple-element.55) | copy-start | bytes 6291460
  254.7 5.0 %copy-start.3 = (bf16[2,8,128,512]{3,2,1,0:T(8,128)(2,1)S(1)}, bf16[2,8,128,512]{3,2,1,0:T(8,128)(2,1)}, u32[]{:S(2)}) copy-start(bf16[2,8,128,512]{3,2,1,0:T(8,128)(2,1)} %get-tuple-element.31) | copy-start | bytes 6291460
  254.7 5.0 %copy-start.4 = (bf16[2,8,128,512]{3,2,1,0:T(8,128)(2,1)S(1)}, bf16[2,8,128,512]{3,2,1,0:T(8,128)(2,1)}, u32[]{:S(2)}) copy-start(bf16[2,8,128,512]{3,2,1,0:T(8,128)(2,1)} %get-tuple-element.32) | copy-start | bytes 6291460
  254.7 5.0 %copy-start.5 = (bf16[2,8,128,512]{3,2,1,0:T(8,128)(2,1)S(1)}, bf16[2,8,128,512]{3,2,1,0:T(8,128)(2,1)}, u32[]{:S(2)}) copy-start(bf16[2,8,128,512]{3,2,1,0:T(8,128)(2,1)} %get-tuple-element.33) | copy-start | bytes 6291460
  263.9 14.8 %copy-start = (bf16[2,8,128,512]{3,2,1,0:T(8,128)(2,1)S(1)}, bf16[2,8,128,512]{3,2,1,0:T(8,128)(2,1)}, u32[]{:S(2)}) copy-start(bf16[2,8,128,512]{3,2,1,0:T(8,128)(2,1)} %param.8) | copy-start | bytes 6291460
  263.9 14.8 %copy-start.28 = (f32[512]{0:T(512)S(1)}, f32[512]{0:T(512)}, u32[]{:S(2)}) copy-start(f32[512]{0:T(512)} %param.13) | copy-start | bytes 6148
  (8 other events, 31.7 us)
